TPU v7x, 256 devices: a whole 4x4x8 slice. The times are simulated.
256 devices in a mesh: group: 8 (over z_lo, y), dev: 32 (over z_hi, x, core).
Axes of the slice: x: 4, y: 4, z: 8 (z_hi: 4, z_lo: 2; z = z_hi * 2 + z_lo), core: 2. Of those that a mesh axis runs over, the one named last changes fastest.
Arguments:
- right_side: float32 [3, 16, 64, 64, 128], P(None, 'group', 'dev'), may hold values from -60 to 60
- stiff_diag: float32 [3, 3, 16, 4096], P(None, None, 'group', 'dev'), may hold values from -0.1 to 12.75, as said below
- stiff_lower: float32 [3, 3, 13, 16, 4096], P(None, None, None, 'group', 'dev'), may hold values from -0.08 to 0.08
- fsai_diag: float32 [3, 3, 16, 4096], P(None, None, 'group', 'dev'), may hold values from -0.1 to 1, as said below
- fsai_lower: float32 [3, 3, 13, 16, 4096], P(None, None, None, 'group', 'dev'), may hold values from -0.12 to 0.12
- fsai_pattern: int32 [13, 16, 4096], P(None, 'group', 'dev'), may hold values 0 or 1
Outputs:
- solution: float32 [3, 16, 64, 64, 128], P(None, 'group', 'dev')
- residual: float32 [3, 16, 64, 64, 128], P(None, 'group', 'dev')
Inputs may be any that keep to these rules, and one draw needn't show every extreme that they name: `stiff_diag`: each 3 by 3 block is symmetric. `fsai_diag`: each 3 by 3 block is zero above its diagonal and positive on it.
All inputs are finite; a program needn't handle non-finite values. No bound on the sum of `fsai_pattern` on one device may be relied on, other than what follows from the above.
Results may differ from a plain program's by a relative error of at most 0.0003.
Values sent between devices are 32-bit elements; how exact they have to be, the bound alone decides.
A program may use at most 128 MiB of HBM per device.

v0:
```python
import jax
import jax.numpy as jnp
from jax import lax
from jax.sharding import PartitionSpec as P

ITERS = 2
highest = lax.Precision.HIGHEST
lower_offsets = [(0, 0, -1), (0, -1, -1), (0, -1, 0), (0, -1, 1)] + [
    (-1, row_step, column_step) for row_step in (-1, 0, 1) for column_step in (-1, 0, 1)
]


def with_halo(block, sides, width):
    for axis, dim in sides:
        count = lax.axis_size(axis)
        forward = [(i, i + 1) for i in range(count - 1)]
        backward = [(target, source) for source, target in forward]
        low = lax.ppermute(
            lax.slice_in_dim(block, block.shape[dim] - width, None, axis=dim), axis, forward
        )
        high = lax.ppermute(lax.slice_in_dim(block, 0, width, axis=dim), axis, backward)
        block = jnp.concatenate([low, block, high], axis=dim)
    return block


def from_behind(value, axis, steps):
    count = lax.axis_size(axis)
    first, last = (max(0, -steps), min(count, count - steps))
    return lax.ppermute(value, axis, [(source, source + steps) for source in range(first, last)])


def block_mul(coeffs, vector):
    return jnp.stack(
        [
            coeffs[target, 0][..., None] * vector[0]
            + coeffs[target, 1][..., None] * vector[1]
            + coeffs[target, 2][..., None] * vector[2]
            for target in range(3)
        ]
    )


def block_mul_transposed(coeffs, vector):
    return jnp.stack(
        [
            coeffs[0, target][..., None] * vector[0]
            + coeffs[1, target][..., None] * vector[1]
            + coeffs[2, target][..., None] * vector[2]
            for target in range(3)
        ]
    )


def pad_columns(vector):
    return jnp.pad(vector, ((0, 0), (0, 0), (0, 0), (1, 1), (0, 0)))


def local_gram(left_block, right_block):
    return jnp.einsum("azxyr,azxys->rs", left_block, right_block, precision=highest)


def combine(vector, coeffs):
    return jnp.einsum("azxyr,rs->azxys", vector, coeffs, precision=highest)


def gram_solve(matrix, right_terms):
    factor = jnp.linalg.cholesky(matrix)
    halfway = lax.linalg.triangular_solve(factor, right_terms, left_side=True, lower=True)
    return lax.linalg.triangular_solve(
        factor, halfway, left_side=True, lower=True, transpose_a=True
    )


def per_device(right_side, stiff_diag, stiff_lower, fsai_diag, fsai_lower, fsai_pattern):
    local_planes = right_side.shape[1]
    local_rows = right_side.shape[2]
    line_length = right_side.shape[3]
    slot_count = stiff_lower.shape[2]
    stiff_d = stiff_diag.reshape(3, 3, local_planes, local_rows, line_length)
    fsai_d = fsai_diag.reshape(3, 3, local_planes, local_rows, line_length)
    stiff_low = stiff_lower.reshape(3, 3, slot_count, local_planes, local_rows, line_length)
    kept = fsai_pattern.astype(jnp.float32)
    fsai_low = (fsai_lower * kept[None, None]).reshape(
        3, 3, slot_count, local_planes, local_rows, line_length
    )

    def lower_window(vector):
        rimmed = with_halo(vector, (("dev", 2),), 1)
        plane_under = from_behind(rimmed[:, local_planes - 1 :], "group", 1)
        return pad_columns(jnp.concatenate([plane_under, rimmed], axis=1))

    def gather_lower(diag_blocks, low_blocks, window_data, vector):
        result = block_mul(diag_blocks, vector)
        for slot_index, (depth_step, row_step, column_step) in enumerate(lower_offsets):
            picked = window_data[
                :,
                1 + depth_step : 1 + depth_step + local_planes,
                1 + row_step : 1 + row_step + local_rows,
                1 + column_step : 1 + column_step + line_length,
            ]
            result = result + block_mul(low_blocks[:, :, slot_index], picked)
        return result

    def push_upper(low_blocks, vector):
        buffer = None
        for slot_index, (depth_step, row_step, column_step) in enumerate(lower_offsets):
            slot_term = block_mul_transposed(low_blocks[:, :, slot_index], vector)
            placed = jnp.pad(
                slot_term,
                (
                    (0, 0),
                    (1 + depth_step, -depth_step),
                    (1 + row_step, 1 - row_step),
                    (1 + column_step, 1 - column_step),
                    (0, 0),
                ),
            )
            buffer = placed if buffer is None else buffer + placed
        inner_part = buffer[:, :, :, 1 : line_length + 1]
        rim_rows = jnp.concatenate(
            [inner_part[:, :, :1], inner_part[:, :, local_rows + 1 :]], axis=2
        )
        arrived = with_halo(rim_rows, (("dev", 2),), 1)
        core_part = inner_part[:, :, 1 : local_rows + 1]
        core_part = core_part.at[:, :, :1].add(arrived[:, :, :1])
        core_part = core_part.at[:, :, local_rows - 1 :].add(arrived[:, :, 3:])
        returned = from_behind(core_part[:, :1], "group", -1)
        return core_part[:, 1:].at[:, local_planes - 1 :].add(returned)

    def apply_fsai(vector):
        return gather_lower(fsai_d, fsai_low, lower_window(vector), vector)

    def apply_fsai_transposed(vector):
        diagonal_part = block_mul_transposed(fsai_d, vector)
        upper_sum = push_upper(fsai_low, vector)
        return diagonal_part + upper_sum

    def residual_sum(weighted):
        return lax.psum(local_gram(weighted, weighted), ("group", "dev"))

    solution = jnp.zeros_like(right_side)
    residual = right_side
    weighted = apply_fsai(residual)
    resid_gram = residual_sum(weighted)
    direction = apply_fsai_transposed(weighted)
    for iteration in range(ITERS):
        lower_sum = gather_lower(stiff_d, stiff_low, lower_window(direction), direction)
        apply_upper_sum = push_upper(stiff_low, direction)
        product = lower_sum + apply_upper_sum
        step_size = gram_solve(
            lax.psum(local_gram(direction, product), ("group", "dev")), resid_gram
        )
        solution = solution + combine(direction, step_size)
        residual = residual - combine(product, step_size)
        if iteration + 1 < ITERS:
            weighted = apply_fsai(residual)
            next_gram = residual_sum(weighted)
            precond = apply_fsai_transposed(weighted)
            conjugacy = gram_solve(resid_gram, next_gram)
            direction = precond + combine(direction, conjugacy)
            resid_gram = next_gram
    return (solution, residual)


def solution(mesh):
    return jax.shard_map(
        per_device,
        mesh=mesh,
        in_specs=(
            P(None, "group", "dev", None, None),
            P(None, None, "group", "dev"),
            P(None, None, None, "group", "dev"),
            P(None, None, "group", "dev"),
            P(None, None, None, "group", "dev"),
            P(None, "group", "dev"),
        ),
        out_specs=(P(None, "group", "dev", None, None), P(None, "group", "dev", None, None)),
        check_vma=False,
    )
```

profile of v0, /device:TPU:1, one launch (start us, length us, event | category | flops | bytes accessed | tf_op | source)
XLA Modules:
  0.0 1071.7 jit_solution(4820610917557618189)
XLA Ops:
  8.3 4.5 collective-permute-start
  12.8 1.9 collective-permute-start.1
  25.8 3.7 collective-permute-start.2
  31.3 5.2 collective-permute-done.2
  63.6 1.4 fusion.48
  65.1 4.8 collective-permute-start.3
  71.4 1.9 collective-permute-start.4
  74.1 5.4 collective-permute-done.4
  79.6 1.3 collective-permute-start.5
  81.5 1.4 convolution_bitcast_fusion.5
  83.0 3.7 collective-permute-done.5
  87.0 3.9 collective-permute-start.6
  90.9 2.1 collective-permute-start.7
  102.7 1.4 fusion.36
  104.2 3.6 collective-permute-start.9
  107.8 1.9 collective-permute-start.10
  109.8 3.9 collective-permute-start.8
  114.2 1.6 collective-permute-done.10
  117.3 4.0 collective-permute-done.8
  126.9 1.4 convolution_bitcast_fusion.6
  128.6 264.0 %all-reduce.65.cloned.1.call-done = (f32[128,128]{0,1:T(8,128)}, f32[128,128]{0,1:T(8,128)}) async-done(((f32[128,128]{0,1:T(8,128)}, f32[128,128]{0,1:T(8,128)}), (f32[128,128]{0,1:T(8,128)}, f32[128,128]{0,1:T(8,128)})) %all-reduce.65.cloned.1.call-update) | async-done | bytes 131088 | tf_op jit(solution)/shard_map/psum | solution.py:139
  394.4 11.7 %cholesky.59 = f32[128,128]{1,0:T(8,128)S(1)} custom-call(f32[128,128]{1,0:T(8,128)S(1)} %fusion.164), custom_call_target="Cholesky" | custom-call | tf_op jit(solution)/shard_map/jit(cholesky)/cholesky | solution.py:67
  407.5 9.8 custom-call.13
  420.2 4.9 collective-permute-start.12
  425.1 1.9 collective-permute-start.13
  427.0 11.7 %cholesky.70 = f32[128,128]{1,0:T(8,128)S(1)} custom-call(f32[128,128]{1,0:T(8,128)S(1)} %fusion.160), custom_call_target="Cholesky" | custom-call | tf_op jit(solution)/shard_map/jit(cholesky)/cholesky | solution.py:67
  440.4 1.8 collective-permute-start.14
  444.2 6.4 collective-permute-done.14
  477.7 1.4 fusion.24
  480.0 3.3 collective-permute-start.15
  483.9 10.4 custom-call.15
  494.3 1.9 collective-permute-start.16
  496.3 1.4 convolution_bitcast_fusion.3
  498.8 3.8 collective-permute-done.16
  505.0 238.5 %all-reduce.61.cloned.1.call-done = f32[128,128]{1,0:T(8,128)} async-done(((f32[128,128]{1,0:T(8,128)}), f32[128,128]{1,0:T(8,128)}) %all-reduce.61.cloned.1.call-update) | async-done | bytes 65552 | tf_op jit(solution)/shard_map/psum | solution.py:139
  756.5 2.5 collective-permute-start.18
  759.0 1.9 collective-permute-start.19
  762.6 1.4 fusion.12
  764.1 4.4 collective-permute-start.21
  768.5 1.9 collective-permute-start.22
  770.5 2.7 collective-permute-start.20
  773.6 2.9 collective-permute-done.22
  776.7 1.5 collective-permute-start.23
  778.2 1.8 collective-permute-done.20
  785.8 1.4 convolution_bitcast_fusion.1
  787.2 249.6 %all-reduce.63.cloned.1.call-done = f32[128,128]{0,1:T(8,128)} async-done(((f32[128,128]{0,1:T(8,128)}), f32[128,128]{0,1:T(8,128)}) %all-reduce.63.cloned.1.call-update) | async-done | bytes 65552 | tf_op jit(solution)/shard_map/psum | solution.py:151
  1038.6 11.7 %cholesky.81 = f32[128,128]{1,0:T(8,128)S(1)} custom-call(f32[128,128]{1,0:T(8,128)S(1)} %fusion.156), custom_call_target="Cholesky" | custom-call | tf_op jit(solution)/shard_map/jit(cholesky)/cholesky | solution.py:67
  1051.7 9.8 custom-call.17
  (785 shorter events, 125.9 us)
Async XLA Ops:
  7.2 385.4 %all-reduce.65.cloned.1.call-start = ((), (), s32[]{:S(2)}) async-start(), calls=%async_computation.2 | async-start | bytes 262144 | tf_op jit(solution)/shard_map/psum | solution.py:139
  8.3 17.4 %collective-permute-start = (f32[3,2,1,64,128]{4,3,2,1,0:T(8,128)S(1)}, f32[3,2,1,64,128]{4,3,2,1,0:T(8,128)S(1)}, u32[]{:S(2)}, u32[]{:S(2)}) collective-permute-start(f32[3,2,1,64,128]{4,3,2,1,0:T(8,128)S(1)} %get-tuple-element.502), channel_id=1, source_target_pairs={{0,1},{1,2},{2,3},{3,4},{4,5},{5,6},{6,7},{7,8},{8,9},{9,10},{10,1... | collective-permute-start | bytes 589832 | tf_op jit(solution)/shard_map/ppermute | solution.py:18
  12.8 13.0 %collective-permute-start.1 = (f32[3,2,1,64,128]{4,3,2,1,0:T(8,128)S(1)}, f32[3,2,1,64,128]{4,3,2,1,0:T(8,128)S(1)}, u32[]{:S(2)}, u32[]{:S(2)}) collective-permute-start(f32[3,2,1,64,128]{4,3,2,1,0:T(8,128)S(1)} %get-tuple-element.501), channel_id=1, source_target_pairs={{1,0},{2,1},{3,2},{4,3},{5,4},{6,5},{7,6},{8,7},{9,8},{10,9},{11,1... | collective-permute-start | bytes 589832 | tf_op jit(solution)/shard_map/ppermute | solution.py:21
  18.4 102.9 %copy-start.17 = (f32[2,2,64]{2,1,0:T(2,128)}, f32[2,2,64]{2,1,0:T(2,128)S(1)}, u32[]{:S(2)}) copy-start(f32[2,2,64]{2,1,0:T(2,128)S(1)} %get-tuple-element.651) | copy-start | bytes 3076
  18.4 103.0 %copy-start.19 = (f32[2,2,64]{2,1,0:T(2,128)}, f32[2,2,64]{2,1,0:T(2,128)S(1)}, u32[]{:S(2)}) copy-start(f32[2,2,64]{2,1,0:T(2,128)S(1)} %get-tuple-element.658) | copy-start | bytes 3076
  18.4 103.0 %copy-start.21 = (f32[2,2,64]{2,1,0:T(2,128)}, f32[2,2,64]{2,1,0:T(2,128)S(1)}, u32[]{:S(2)}) copy-start(f32[2,2,64]{2,1,0:T(2,128)S(1)} %get-tuple-element.659) | copy-start | bytes 3076
  18.4 103.4 %copy-start.11 = (f32[2,2,64]{2,1,0:T(2,128)}, f32[2,2,64]{2,1,0:T(2,128)S(1)}, u32[]{:S(2)}) copy-start(f32[2,2,64]{2,1,0:T(2,128)S(1)} %get-tuple-element.655) | copy-start | bytes 3076
  18.4 103.4 %copy-start.13 = (f32[2,2,64]{2,1,0:T(2,128)}, f32[2,2,64]{2,1,0:T(2,128)S(1)}, u32[]{:S(2)}) copy-start(f32[2,2,64]{2,1,0:T(2,128)S(1)} %get-tuple-element.656) | copy-start | bytes 3076
  18.5 103.4 %copy-start.15 = (f32[2,2,64]{2,1,0:T(2,128)}, f32[2,2,64]{2,1,0:T(2,128)S(1)}, u32[]{:S(2)}) copy-start(f32[2,2,64]{2,1,0:T(2,128)S(1)} %get-tuple-element.657) | copy-start | bytes 3076
  18.5 104.0 %copy-start.5 = (f32[2,2,64]{2,1,0:T(2,128)}, f32[2,2,64]{2,1,0:T(2,128)S(1)}, u32[]{:S(2)}) copy-start(f32[2,2,64]{2,1,0:T(2,128)S(1)} %get-tuple-element.652) | copy-start | bytes 3076
  18.5 104.0 %copy-start.7 = (f32[2,2,64]{2,1,0:T(2,128)}, f32[2,2,64]{2,1,0:T(2,128)S(1)}, u32[]{:S(2)}) copy-start(f32[2,2,64]{2,1,0:T(2,128)S(1)} %get-tuple-element.653) | copy-start | bytes 3076
  18.5 104.0 %copy-start.9 = (f32[2,2,64]{2,1,0:T(2,128)}, f32[2,2,64]{2,1,0:T(2,128)S(1)}, u32[]{:S(2)}) copy-start(f32[2,2,64]{2,1,0:T(2,128)S(1)} %get-tuple-element.654) | copy-start | bytes 3076
  23.2 102.1 %copy-start.25 = (f32[2,2,64]{2,1,0:T(2,128)}, f32[2,2,64]{2,1,0:T(2,128)S(1)}, u32[]{:S(2)}) copy-start(f32[2,2,64]{2,1,0:T(2,128)S(1)} %get-tuple-element.637) | copy-start | bytes 3076
  23.2 102.1 %copy-start.27 = (f32[2,2,64]{2,1,0:T(2,128)}, f32[2,2,64]{2,1,0:T(2,128)S(1)}, u32[]{:S(2)}) copy-start(f32[2,2,64]{2,1,0:T(2,128)S(1)} %get-tuple-element.638) | copy-start | bytes 3076
  23.2 102.1 %copy-start.29 = (f32[2,2,64]{2,1,0:T(2,128)}, f32[2,2,64]{2,1,0:T(2,128)S(1)}, u32[]{:S(2)}) copy-start(f32[2,2,64]{2,1,0:T(2,128)S(1)} %get-tuple-element.639) | copy-start | bytes 3076
  23.2 102.1 %copy-start.31 = (f32[2,2,64]{2,1,0:T(2,128)}, f32[2,2,64]{2,1,0:T(2,128)S(1)}, u32[]{:S(2)}) copy-start(f32[2,2,64]{2,1,0:T(2,128)S(1)} %get-tuple-element.640) | copy-start | bytes 3076
  23.2 102.1 %copy-start.33 = (f32[2,2,64]{2,1,0:T(2,128)}, f32[2,2,64]{2,1,0:T(2,128)S(1)}, u32[]{:S(2)}) copy-start(f32[2,2,64]{2,1,0:T(2,128)S(1)} %get-tuple-element.641) | copy-start | bytes 3076
  23.2 102.1 %copy-start.35 = (f32[2,2,64]{2,1,0:T(2,128)}, f32[2,2,64]{2,1,0:T(2,128)S(1)}, u32[]{:S(2)}) copy-start(f32[2,2,64]{2,1,0:T(2,128)S(1)} %get-tuple-element.851) | copy-start | bytes 3076
  23.2 102.1 %copy-start.37 = (f32[2,2,64]{2,1,0:T(2,128)}, f32[2,2,64]{2,1,0:T(2,128)S(1)}, u32[]{:S(2)}) copy-start(f32[2,2,64]{2,1,0:T(2,128)S(1)} %get-tuple-element.852) | copy-start | bytes 3076
  23.2 102.1 %copy-start.39 = (f32[2,2,64]{2,1,0:T(2,128)}, f32[2,2,64]{2,1,0:T(2,128)S(1)}, u32[]{:S(2)}) copy-start(f32[2,2,64]{2,1,0:T(2,128)S(1)} %get-tuple-element.853) | copy-start | bytes 3076
  23.2 102.1 %copy-start.41 = (f32[2,2,64]{2,1,0:T(2,128)}, f32[2,2,64]{2,1,0:T(2,128)S(1)}, u32[]{:S(2)}) copy-start(f32[2,2,64]{2,1,0:T(2,128)S(1)} %get-tuple-element.854) | copy-start | bytes 3076
  23.3 102.1 %copy-start.43 = (f32[2,2,64]{2,1,0:T(2,128)}, f32[2,2,64]{2,1,0:T(2,128)S(1)}, u32[]{:S(2)}) copy-start(f32[2,2,64]{2,1,0:T(2,128)S(1)} %get-tuple-element.855) | copy-start | bytes 3076
  25.8 10.7 collective-permute-start.2
  65.1 8.9 collective-permute-start.3
  71.4 8.0 collective-permute-start.4
  79.6 7.2 collective-permute-start.5
  87.0 14.7 %collective-permute-start.6 = (f32[3,2,1,64,128]{4,3,2,1,0:T(8,128)S(1)}, f32[3,2,1,64,128]{4,3,2,1,0:T(8,128)S(1)}, u32[]{:S(2)}, u32[]{:S(2)}) collective-permute-start(f32[3,2,1,64,128]{4,3,2,1,0:T(8,128)S(1)} %get-tuple-element.416), channel_id=1, source_target_pairs={{0,1},{1,2},{2,3},{3,4},{4,5},{5,6},{6,7},{7,8},{8,9},{9,10},{10,1... | collective-permute-start | bytes 589832 | tf_op jit(solution)/shard_map/ppermute | solution.py:18
  90.9 18.8 %collective-permute-start.7 = (f32[3,2,1,64,128]{4,3,2,1,0:T(8,128)S(1)}, f32[3,2,1,64,128]{4,3,2,1,0:T(8,128)S(1)}, u32[]{:S(2)}, u32[]{:S(2)}) collective-permute-start(f32[3,2,1,64,128]{4,3,2,1,0:T(8,128)S(1)} %get-tuple-element.417), channel_id=1, source_target_pairs={{1,0},{2,1},{3,2},{4,3},{5,4},{6,5},{7,6},{8,7},{9,8},{10,9},{11,1... | collective-permute-start | bytes 589832 | tf_op jit(solution)/shard_map/ppermute | solution.py:21
  104.2 10.0 collective-permute-start.9
  107.8 8.0 collective-permute-start.10
  109.8 11.5 %collective-permute-start.8 = (f32[3,1,4,64,128]{4,3,2,1,0:T(8,128)S(1)}, f32[3,1,4,64,128]{4,3,2,1,0:T(8,128)S(1)}, u32[]{:S(2)}, u32[]{:S(2)}) collective-permute-start(f32[3,1,4,64,128]{4,3,2,1,0:T(8,128)S(1)} %pad_maximum_fusion.5), channel_id=1, source_target_pairs={{0,32},{32,64},{64,96},{96,128},{128,160},{160,192},{192,224},{1,3... | collective-permute-start | bytes 1179656 | tf_op jit(solution)/shard_map/ppermute | solution.py:29
  116.0 10.2 collective-permute-start.11
  128.4 615.1 %all-reduce.61.cloned.1.call-start = ((), (), s32[]{:S(2)}) async-start(), calls=%async_computation | async-start | bytes 131072 | tf_op jit(solution)/shard_map/psum | solution.py:139
  420.2 20.2 %collective-permute-start.12 = (f32[3,2,1,64,128]{4,3,2,1,0:T(8,128)S(1)}, f32[3,2,1,64,128]{4,3,2,1,0:T(8,128)S(1)}, u32[]{:S(2)}, u32[]{:S(2)}) collective-permute-start(f32[3,2,1,64,128]{4,3,2,1,0:T(8,128)S(1)} %get-tuple-element.410), channel_id=1, source_target_pairs={{0,1},{1,2},{2,3},{3,4},{4,5},{5,6},{6,7},{7,8},{8,9},{9,10},{10,1... | collective-permute-start | bytes 589832 | tf_op jit(solution)/shard_map/ppermute | solution.py:18
  425.1 15.3 %collective-permute-start.13 = (f32[3,2,1,64,128]{4,3,2,1,0:T(8,128)S(1)}, f32[3,2,1,64,128]{4,3,2,1,0:T(8,128)S(1)}, u32[]{:S(2)}, u32[]{:S(2)}) collective-permute-start(f32[3,2,1,64,128]{4,3,2,1,0:T(8,128)S(1)} %get-tuple-element.411), channel_id=1, source_target_pairs={{1,0},{2,1},{3,2},{4,3},{5,4},{6,5},{7,6},{8,7},{9,8},{10,9},{11,1... | collective-permute-start | bytes 589832 | tf_op jit(solution)/shard_map/ppermute | solution.py:21
  440.4 10.2 collective-permute-start.14
  480.0 17.8 %collective-permute-start.15 = (f32[3,3,1,64,128]{4,3,2,1,0:T(8,128)}, f32[3,3,1,64,128]{4,3,2,1,0:T(8,128)}, u32[]{:S(2)}, u32[]{:S(2)}) collective-permute-start(f32[3,3,1,64,128]{4,3,2,1,0:T(8,128)} %get-tuple-element.166), channel_id=1, source_target_pairs={{0,1},{1,2},{2,3},{3,4},{4,5},{5,6},{6,7},{7,8},{8,9},{9,10},{10,1... | collective-permute-start | bytes 884744 | tf_op jit(solution)/shard_map/ppermute | solution.py:18
  494.3 8.3 collective-permute-start.16
  497.7 245.8 %copy-start.3 = (f32[1,128,128]{1,2,0:T(8,128)S(1)}, f32[1,128,128]{1,2,0:T(8,128)}, u32[]{:S(2)}) copy-start(f32[1,128,128]{1,2,0:T(8,128)} %custom-call.15) | copy-start | bytes 196612
  497.8 539.1 %all-reduce.63.cloned.1.call-start = ((), (), s32[]{:S(2)}) async-start(), calls=%async_computation.1 | async-start | bytes 131072 | tf_op jit(solution)/shard_map/psum | solution.py:151
  503.7 241.2 %collective-permute-start.17 = (f32[3,1,2,64,128]{4,3,2,1,0:T(8,128)S(1)}, f32[3,1,2,64,128]{4,3,2,1,0:T(8,128)S(1)}, u32[]{:S(2)}, u32[]{:S(2)}) collective-permute-start(f32[3,1,2,64,128]{4,3,2,1,0:T(8,128)S(1)} %slice.4621), channel_id=1, source_target_pairs={{32,0},{64,32},{96,64},{128,96},{160,128},{192,160},{224,192},{33,... | collective-permute-start | bytes 589832 | tf_op jit(solution)/shard_map/ppermute | solution.py:29
  756.5 5.1 collective-permute-start.18
  759.0 11.4 %collective-permute-start.19 = (f32[3,2,1,64,128]{4,3,2,1,0:T(8,128)S(1)}, f32[3,2,1,64,128]{4,3,2,1,0:T(8,128)S(1)}, u32[]{:S(2)}, u32[]{:S(2)}) collective-permute-start(f32[3,2,1,64,128]{4,3,2,1,0:T(8,128)S(1)} %get-tuple-element.325), channel_id=1, source_target_pairs={{1,0},{2,1},{3,2},{4,3},{5,4},{6,5},{7,6},{8,7},{9,8},{10,9},{11,1... | collective-permute-start | bytes 589832 | tf_op jit(solution)/shard_map/ppermute | solution.py:21
  764.1 9.5 collective-permute-start.21
  768.5 8.0 collective-permute-start.22
  770.5 9.5 collective-permute-start.20
  776.7 8.3 collective-permute-start.23
  785.8 275.7 %copy-start.2 = (f32[128,128]{1,0:T(8,128)S(1)}, f32[128,128]{1,0:T(8,128)}, u32[]{:S(2)}) copy-start(f32[128,128]{1,0:T(8,128)} %all-reduce.61.cloned.1.call-done) | copy-start | bytes 196612
  (259 other events, 2389.0 us)
Sparse Core Ops, SparseCore 0:
  128.5 264.0 all-reduce.64
  497.9 245.5 all-reduce.60
  787.4 249.4 all-reduce.62
where the time goes:
time: 1080 us; the launch traced here: 1070 us
  waiting for transfers between devices  788 us (73%)
  other arithmetic  168 us (16%)
  starting transfers between devices  65.3 us (6%)
  between operations  19.7 us (2%)
  local copies, waits for them, and re-layouts  17.9 us (2%)
  matrix products  12.7 us (1%)
    psum x2, waiting for transfers between devices, residual_sum(): return lax.psum(local_gram(weighted, weighted), ('group', 'dev'))  502 us
    psum x1, waiting for transfers between devices, per_device(): lax.psum(local_gram(direction, product), ('group', 'dev'))  250 us
    add x55, other arithmetic, block_mul(): coeffs[target, 0][..., None] * vector[0]  42.9 us
    add x50, other arithmetic, block_mul_transposed(): coeffs[0, target][..., None] * vector[0]  41.6 us
    another operation x9, other arithmetic, gram_solve(): factor = jnp.linalg.cholesky(matrix)  37.2 us
    ppermute x8, starting transfers between devices, with_halo(): lax.ppermute(lax.slice_in_dim(block, block.shape[dim] - width, None, axis...  32 us
    another operation x6, other arithmetic, gram_solve(): lax.linalg.triangular_solve(factor, halfway, left_side=True, lower=True,...  32 us
  transfers between devices with their start and end apart: 27, of which 13 were waited for; matrix products, arithmetic and copies ran while one was open for 7% of the time, Pallas kernels for 0%

commit v1 on v0

--- a/solution.py
+++ b/solution.py
@@ -1,3 +1,4 @@
+import functools
 import jax
 import jax.numpy as jnp
 from jax import lax
@@ -8,6 +9,15 @@
 lower_offsets = [(0, 0, -1), (0, -1, -1), (0, -1, 0), (0, -1, 1)] + [
     (-1, row_step, column_step) for row_step in (-1, 0, 1) for column_step in (-1, 0, 1)
 ]
+
+
+def indices_post(inner_x, a_name, across):
+    for dev_i in (a_name, across):
+        inner_x = lax.psum(inner_x, axis_name=dev_i)
+    return inner_x
+
+
+series_all_push = functools.partial(indices_post, a_name="group", across="dev")
 
 
 def with_halo(block, sides, width):
@@ -147,9 +157,7 @@
         lower_sum = gather_lower(stiff_d, stiff_low, lower_window(direction), direction)
         apply_upper_sum = push_upper(stiff_low, direction)
         product = lower_sum + apply_upper_sum
-        step_size = gram_solve(
-            lax.psum(local_gram(direction, product), ("group", "dev")), resid_gram
-        )
+        step_size = gram_solve(series_all_push(local_gram(direction, product)), resid_gram)
         solution = solution + combine(direction, step_size)
         residual = residual - combine(product, step_size)
         if iteration + 1 < ITERS:

time: 1080 us -> 1490 us (1.38)
  waiting for transfers between devices: 788 us -> 1200 us
    psum x1 -> x4, waiting for transfers between devices: 250 us -> 679 us  [indices_post(): inner_x = lax.psum(inner_x, axis_name=dev_i)]
  transfers between devices with their start and end apart: 27 -> 30, of which waited for: 13 -> 15; matrix products, arithmetic and copies ran while one was open for 7% -> 5% of each run, Pallas kernels for 0% -> 0%
where the time goes in v1:
time: 1490 us; the launch traced here: 1480 us
  waiting for transfers between devices  1200 us (81%)
  other arithmetic  167 us (11%)
  starting transfers between devices  65.3 us (4%)
  between operations  22.1 us (1%)
  local copies, waits for them, and re-layouts  18.3 us (1%)
    psum x4, waiting for transfers between devices, indices_post(): inner_x = lax.psum(inner_x, axis_name=dev_i)  679 us
    psum x2, waiting for transfers between devices, residual_sum(): return lax.psum(local_gram(weighted, weighted), ('group', 'dev'))  493 us
    add x50, other arithmetic, block_mul_transposed(): coeffs[0, target][..., None] * vector[0]  41.6 us
    add x55, other arithmetic, block_mul(): coeffs[target, 0][..., None] * vector[0]  40.3 us
    another operation x9, other arithmetic, gram_solve(): factor = jnp.linalg.cholesky(matrix)  37.2 us
    another operation x6, other arithmetic, gram_solve(): lax.linalg.triangular_solve(factor, halfway, left_side=True, lower=True,...  32 us
  transfers between devices with their start and end apart: 30, of which 15 were waited for; matrix products, arithmetic and copies ran while one was open for 5% of the time, Pallas kernels for 0%

profile of v1, /device:TPU:1, one launch (start us, length us, event | category | flops | bytes accessed | tf_op | source)
XLA Modules:
  0.0 1481.8 jit_solution(6981686148860832715)
XLA Ops:
  9.1 4.5 collective-permute-start
  13.6 1.9 collective-permute-start.1
  27.4 3.7 collective-permute-start.2
  32.9 5.2 collective-permute-done.2
  65.3 1.4 fusion.48
  67.6 4.8 collective-permute-start.3
  72.5 1.9 collective-permute-start.4
  76.6 247.9 %all-reduce.67.cloned.1.call-done = f32[128,128]{0,1:T(8,128)} async-done(((f32[128,128]{0,1:T(8,128)}), f32[128,128]{0,1:T(8,128)}) %all-reduce.67.cloned.1.call-update) | async-done | bytes 65552 | tf_op jit(solution)/shard_map/psum | solution.py:149
  326.6 1.5 collective-permute-start.5
  328.1 11.7 cholesky.70
  340.2 2.5 collective-permute-start.6
  342.6 1.9 collective-permute-start.7
  353.8 1.4 fusion.36
  355.3 3.6 collective-permute-start.9
  359.0 1.9 collective-permute-start.10
  360.9 4.3 collective-permute-start.8
  367.1 1.5 collective-permute-start.11
  368.7 4.1 collective-permute-done.8
  378.4 1.4 convolution_bitcast_fusion.6
  379.9 79.8 %all-reduce.63.cloned.1.call-done = f32[128,128]{0,1:T(8,128)} async-done(((f32[128,128]{0,1:T(8,128)}), f32[128,128]{0,1:T(8,128)}) %all-reduce.63.cloned.1.call-update) | async-done | bytes 65552 | tf_op jit(solution)/shard_map/psum | solution.py:16
  460.5 258.1 %all-reduce.65.cloned.1.call-done = f32[128,128]{0,1:T(8,128)} async-done(((f32[128,128]{0,1:T(8,128)}), f32[128,128]{0,1:T(8,128)}) %all-reduce.65.cloned.1.call-update) | async-done | bytes 65552 | tf_op jit(solution)/shard_map/psum | solution.py:16
  720.4 11.7 cholesky.59
  733.5 9.8 custom-call.13
  744.4 1.9 collective-permute-start.12
  746.3 3.8 collective-permute-start.13
  750.5 2.8 collective-permute-done.13
  753.3 3.5 collective-permute-start.14
  758.9 4.9 collective-permute-done.14
  790.9 1.4 fusion.24
  793.3 2.1 collective-permute-start.15
  796.0 10.4 custom-call.15
  806.4 3.1 collective-permute-start.16
  812.1 2.6 collective-permute-done.16
  817.1 244.7 %all-reduce.69.cloned.1.call-done = f32[128,128]{1,0:T(8,128)} async-done(((f32[128,128]{1,0:T(8,128)}), f32[128,128]{1,0:T(8,128)}) %all-reduce.69.cloned.1.call-update) | async-done | bytes 65552 | tf_op jit(solution)/shard_map/psum | solution.py:149
  1074.8 2.5 collective-permute-start.18
  1077.3 1.9 collective-permute-start.19
  1080.3 1.4 fusion.12
  1081.8 4.4 collective-permute-start.21
  1086.2 1.9 collective-permute-start.22
  1088.1 2.7 collective-permute-start.20
  1091.3 2.9 collective-permute-done.22
  1094.3 1.5 collective-permute-start.23
  1095.9 1.8 collective-permute-done.20
  1103.4 1.4 convolution_bitcast_fusion.1
  1105.2 81.7 %all-reduce.71.cloned.1.call-done = f32[128,128]{0,1:T(8,128)} async-done(((f32[128,128]{0,1:T(8,128)}), f32[128,128]{0,1:T(8,128)}) %all-reduce.71.cloned.1.call-update) | async-done | bytes 65552 | tf_op jit(solution)/shard_map/psum | solution.py:16
  1186.9 259.0 %all-reduce.73.cloned.1.call-done = f32[128,128]{0,1:T(8,128)} async-done(((f32[128,128]{0,1:T(8,128)}), f32[128,128]{0,1:T(8,128)}) %all-reduce.73.cloned.1.call-update) | async-done | bytes 65552 | tf_op jit(solution)/shard_map/psum | solution.py:16
  1447.6 11.7 cholesky.81
  1460.7 9.8 custom-call.17
  (824 shorter events, 126.9 us)
Async XLA Ops:
  8.0 316.4 %all-reduce.67.cloned.1.call-start = ((), (), s32[]{:S(2)}) async-start(), calls=%async_computation.2 | async-start | bytes 131072 | tf_op jit(solution)/shard_map/psum | solution.py:149
  9.1 18.1 %collective-permute-start = (f32[3,2,1,64,128]{4,3,2,1,0:T(8,128)S(1)}, f32[3,2,1,64,128]{4,3,2,1,0:T(8,128)S(1)}, u32[]{:S(2)}, u32[]{:S(2)}) collective-permute-start(f32[3,2,1,64,128]{4,3,2,1,0:T(8,128)S(1)} %get-tuple-element.500), channel_id=1, source_target_pairs={{0,1},{1,2},{2,3},{3,4},{4,5},{5,6},{6,7},{7,8},{8,9},{9,10},{10,1... | collective-permute-start | bytes 589832 | tf_op jit(solution)/shard_map/ppermute | solution.py:28
  13.6 13.7 collective-permute-start.1
  19.3 353.5 %copy-start.19 = (f32[2,2,64]{2,1,0:T(2,128)}, f32[2,2,64]{2,1,0:T(2,128)S(1)}, u32[]{:S(2)}) copy-start(f32[2,2,64]{2,1,0:T(2,128)S(1)} %get-tuple-element.649) | copy-start | bytes 3076
  19.3 353.5 %copy-start.21 = (f32[2,2,64]{2,1,0:T(2,128)}, f32[2,2,64]{2,1,0:T(2,128)S(1)}, u32[]{:S(2)}) copy-start(f32[2,2,64]{2,1,0:T(2,128)S(1)} %get-tuple-element.656) | copy-start | bytes 3076
  19.3 353.5 %copy-start.23 = (f32[2,2,64]{2,1,0:T(2,128)}, f32[2,2,64]{2,1,0:T(2,128)S(1)}, u32[]{:S(2)}) copy-start(f32[2,2,64]{2,1,0:T(2,128)S(1)} %get-tuple-element.657) | copy-start | bytes 3076
  19.3 354.0 %copy-start.13 = (f32[2,2,64]{2,1,0:T(2,128)}, f32[2,2,64]{2,1,0:T(2,128)S(1)}, u32[]{:S(2)}) copy-start(f32[2,2,64]{2,1,0:T(2,128)S(1)} %get-tuple-element.653) | copy-start | bytes 3076
  19.4 354.0 %copy-start.15 = (f32[2,2,64]{2,1,0:T(2,128)}, f32[2,2,64]{2,1,0:T(2,128)S(1)}, u32[]{:S(2)}) copy-start(f32[2,2,64]{2,1,0:T(2,128)S(1)} %get-tuple-element.654) | copy-start | bytes 3076
  19.4 354.0 %copy-start.17 = (f32[2,2,64]{2,1,0:T(2,128)}, f32[2,2,64]{2,1,0:T(2,128)S(1)}, u32[]{:S(2)}) copy-start(f32[2,2,64]{2,1,0:T(2,128)S(1)} %get-tuple-element.655) | copy-start | bytes 3076
  19.4 354.6 %copy-start.7 = (f32[2,2,64]{2,1,0:T(2,128)}, f32[2,2,64]{2,1,0:T(2,128)S(1)}, u32[]{:S(2)}) copy-start(f32[2,2,64]{2,1,0:T(2,128)S(1)} %get-tuple-element.650) | copy-start | bytes 3076
  19.4 354.6 %copy-start.9 = (f32[2,2,64]{2,1,0:T(2,128)}, f32[2,2,64]{2,1,0:T(2,128)S(1)}, u32[]{:S(2)}) copy-start(f32[2,2,64]{2,1,0:T(2,128)S(1)} %get-tuple-element.651) | copy-start | bytes 3076
  19.4 354.6 %copy-start.11 = (f32[2,2,64]{2,1,0:T(2,128)}, f32[2,2,64]{2,1,0:T(2,128)S(1)}, u32[]{:S(2)}) copy-start(f32[2,2,64]{2,1,0:T(2,128)S(1)} %get-tuple-element.652) | copy-start | bytes 3076
  24.1 352.7 %copy-start.29 = (f32[2,2,64]{2,1,0:T(2,128)}, f32[2,2,64]{2,1,0:T(2,128)S(1)}, u32[]{:S(2)}) copy-start(f32[2,2,64]{2,1,0:T(2,128)S(1)} %get-tuple-element.636) | copy-start | bytes 3076
  24.1 352.7 %copy-start.31 = (f32[2,2,64]{2,1,0:T(2,128)}, f32[2,2,64]{2,1,0:T(2,128)S(1)}, u32[]{:S(2)}) copy-start(f32[2,2,64]{2,1,0:T(2,128)S(1)} %get-tuple-element.637) | copy-start | bytes 3076
  24.1 352.7 %copy-start.33 = (f32[2,2,64]{2,1,0:T(2,128)}, f32[2,2,64]{2,1,0:T(2,128)S(1)}, u32[]{:S(2)}) copy-start(f32[2,2,64]{2,1,0:T(2,128)S(1)} %get-tuple-element.638) | copy-start | bytes 3076
  24.1 352.7 %copy-start.35 = (f32[2,2,64]{2,1,0:T(2,128)}, f32[2,2,64]{2,1,0:T(2,128)S(1)}, u32[]{:S(2)}) copy-start(f32[2,2,64]{2,1,0:T(2,128)S(1)} %get-tuple-element.639) | copy-start | bytes 3076
  24.1 352.7 %copy-start.37 = (f32[2,2,64]{2,1,0:T(2,128)}, f32[2,2,64]{2,1,0:T(2,128)S(1)}, u32[]{:S(2)}) copy-start(f32[2,2,64]{2,1,0:T(2,128)S(1)} %get-tuple-element.849) | copy-start | bytes 3076
  24.2 352.7 %copy-start.39 = (f32[2,2,64]{2,1,0:T(2,128)}, f32[2,2,64]{2,1,0:T(2,128)S(1)}, u32[]{:S(2)}) copy-start(f32[2,2,64]{2,1,0:T(2,128)S(1)} %get-tuple-element.850) | copy-start | bytes 3076
  24.2 352.7 %copy-start.41 = (f32[2,2,64]{2,1,0:T(2,128)}, f32[2,2,64]{2,1,0:T(2,128)S(1)}, u32[]{:S(2)}) copy-start(f32[2,2,64]{2,1,0:T(2,128)S(1)} %get-tuple-element.851) | copy-start | bytes 3076
  24.2 352.7 %copy-start.43 = (f32[2,2,64]{2,1,0:T(2,128)}, f32[2,2,64]{2,1,0:T(2,128)S(1)}, u32[]{:S(2)}) copy-start(f32[2,2,64]{2,1,0:T(2,128)S(1)} %get-tuple-element.852) | copy-start | bytes 3076
  27.4 10.7 collective-permute-start.2
  67.6 257.8 %collective-permute-start.3 = (f32[3,3,1,64,128]{4,3,2,1,0:T(8,128)}, f32[3,3,1,64,128]{4,3,2,1,0:T(8,128)}, u32[]{:S(2)}, u32[]{:S(2)}) collective-permute-start(f32[3,3,1,64,128]{4,3,2,1,0:T(8,128)} %get-tuple-element.168), channel_id=1, source_target_pairs={{0,1},{1,2},{2,3},{3,4},{4,5},{5,6},{6,7},{7,8},{8,9},{9,10},{10,1... | collective-permute-start | bytes 884744 | tf_op jit(solution)/shard_map/ppermute | solution.py:28
  72.5 254.0 %collective-permute-start.4 = (f32[3,3,1,64,128]{4,3,2,1,0:T(8,128)}, f32[3,3,1,64,128]{4,3,2,1,0:T(8,128)S(1)}, u32[]{:S(2)}, u32[]{:S(2)}) collective-permute-start(f32[3,3,1,64,128]{4,3,2,1,0:T(8,128)} %get-tuple-element.167), channel_id=1, source_target_pairs={{1,0},{2,1},{3,2},{4,3},{5,4},{6,5},{7,6},{8,7},{9,8},{10,9},{11,1... | collective-permute-start | bytes 884744 | tf_op jit(solution)/shard_map/ppermute | solution.py:31
  75.8 383.9 %all-reduce.63.cloned.1.call-start = ((), (), s32[]{:S(2)}) async-start(), calls=%async_computation | async-start | bytes 131072 | tf_op jit(solution)/shard_map/psum | solution.py:16
  326.6 13.3 collective-permute-start.5
  340.2 13.3 collective-permute-start.6
  342.6 18.3 %collective-permute-start.7 = (f32[3,2,1,64,128]{4,3,2,1,0:T(8,128)S(1)}, f32[3,2,1,64,128]{4,3,2,1,0:T(8,128)S(1)}, u32[]{:S(2)}, u32[]{:S(2)}) collective-permute-start(f32[3,2,1,64,128]{4,3,2,1,0:T(8,128)S(1)} %get-tuple-element.415), channel_id=1, source_target_pairs={{1,0},{2,1},{3,2},{4,3},{5,4},{6,5},{7,6},{8,7},{9,8},{10,9},{11,1... | collective-permute-start | bytes 589832 | tf_op jit(solution)/shard_map/ppermute | solution.py:31
  355.3 10.3 collective-permute-start.9
  359.0 8.0 collective-permute-start.10
  360.9 11.8 collective-permute-start.8
  367.1 10.5 collective-permute-start.11
  379.8 338.8 %all-reduce.65.cloned.1.call-start = ((), (), s32[]{:S(2)}) async-start(), calls=%async_computation.1 | async-start | bytes 131072 | tf_op jit(solution)/shard_map/psum | solution.py:16
  459.8 602.0 %all-reduce.69.cloned.1.call-start = ((), (), s32[]{:S(2)}) async-start(), calls=%async_computation.3 | async-start | bytes 131072 | tf_op jit(solution)/shard_map/psum | solution.py:149
  744.4 6.1 collective-permute-start.12
  746.3 7.0 collective-permute-start.13
  753.3 10.5 collective-permute-start.14
  793.3 17.9 %collective-permute-start.15 = (f32[3,3,1,64,128]{4,3,2,1,0:T(8,128)}, f32[3,3,1,64,128]{4,3,2,1,0:T(8,128)}, u32[]{:S(2)}, u32[]{:S(2)}) collective-permute-start(f32[3,3,1,64,128]{4,3,2,1,0:T(8,128)} %get-tuple-element.164), channel_id=1, source_target_pairs={{0,1},{1,2},{2,3},{3,4},{4,5},{5,6},{6,7},{7,8},{8,9},{9,10},{10,1... | collective-permute-start | bytes 884744 | tf_op jit(solution)/shard_map/ppermute | solution.py:28
  806.4 8.3 collective-permute-start.16
  811.1 375.8 %all-reduce.71.cloned.1.call-start = ((), (), s32[]{:S(2)}) async-start(), calls=%async_computation.4 | async-start | bytes 131072 | tf_op jit(solution)/shard_map/psum | solution.py:16
  815.8 247.4 %collective-permute-start.17 = (f32[3,1,2,64,128]{4,3,2,1,0:T(8,128)S(1)}, f32[3,1,2,64,128]{4,3,2,1,0:T(8,128)S(1)}, u32[]{:S(2)}, u32[]{:S(2)}) collective-permute-start(f32[3,1,2,64,128]{4,3,2,1,0:T(8,128)S(1)} %slice.4621), channel_id=1, source_target_pairs={{32,0},{64,32},{96,64},{128,96},{160,128},{192,160},{224,192},{33,... | collective-permute-start | bytes 589832 | tf_op jit(solution)/shard_map/ppermute | solution.py:39
  1074.8 5.1 collective-permute-start.18
  1077.3 10.8 collective-permute-start.19
  1081.8 9.5 collective-permute-start.21
  1086.2 8.0 collective-permute-start.22
  1088.1 9.5 collective-permute-start.20
  1094.3 8.3 collective-permute-start.23
  1103.4 367.1 %copy-start.2 = (f32[128,128]{1,0:T(8,128)S(1)}, f32[128,128]{1,0:T(8,128)}, u32[]{:S(2)}) copy-start(f32[128,128]{1,0:T(8,128)} %all-reduce.69.cloned.1.call-done) | copy-start | bytes 196612
  1104.9 341.0 %all-reduce.73.cloned.1.call-start = ((), (), s32[]{:S(2)}) async-start(), calls=%async_computation.5 | async-start | bytes 131072 | tf_op jit(solution)/shard_map/psum | solution.py:16
  (277 other events, 2721.4 us)
Sparse Core Ops, SparseCore 0:
  75.9 248.4 all-reduce.66
  811.2 250.5 all-reduce.68
Sparse Core Ops, SparseCore 1:
  379.9 79.8 all-reduce.62
  462.3 256.3 all-reduce.64
  1104.9 81.8 all-reduce.70
  1189.5 256.3 all-reduce.72
